TPU v7x, 512 devices: a whole 4x8x8 slice. The times are simulated.
512 devices in a mesh: ctx: 32 (over z, x), ch: 16 (over y, core).
Axes of the slice: x: 4, y: 8, z: 8, core: 2. Of those that a mesh axis runs over, the one named last changes fastest.
Arguments:
- query_seq: bfloat16 [4096, 4096], P('ctx', 'ch'), may hold values from -6 to 6
- key_seq: bfloat16 [4096, 4096], P('ctx', 'ch'), may hold values from -6 to 6
- value_seq: bfloat16 [4096, 4096], P('ctx', 'ch'), may hold values from -6 to 6
- out_grad: bfloat16 [4096, 4096], P('ctx', 'ch'), may hold values from -6 to 6
- filters: bfloat16 [4096, 256], P('ctx', 'ch'), may hold values from -6 to 6
- skip_gain: float32 [4096], P('ch'), may hold values from -1 to 1
- reaches: int32 [256], P('ch'), may hold values from 1 to 32, as said below
Outputs:
- mixed: bfloat16 [4096, 4096], P('ctx', 'ch')
- query_grad: bfloat16 [4096, 4096], P('ctx', 'ch')
- key_grad: bfloat16 [4096, 4096], P('ctx', 'ch')
- value_grad: bfloat16 [4096, 4096], P('ctx', 'ch')
- filter_grad: float32 [4096, 256], P('ctx', 'ch')
- skip_grad: float32 [4096], P('ch')
Inputs may be any that keep to these rules, and one draw needn't show every extreme that they name: Each group's reach counts its own span; some group reaches the whole context and some group only its own span.
All inputs are finite; a program needn't handle non-finite values.
Results may differ from a plain program's by a relative error of at most 0.01.
Values may be sent and summed in bfloat16 or wider, within the bound.
No kernel may reach another device: no remote copies, remote signals or barrier semaphores. Data moves between devices by JAX's collectives and lax.ppermute only.
A program may use at most 64 MiB of HBM per device.

v0:
```python
import math
import jax
import jax.numpy as jnp
from jax import lax
from jax.sharding import PartitionSpec as P

GROUP = 16


def toeplitz(window):
    size_two, groups = window.shape
    block_len = size_two // 2
    flipped = window[::-1].T
    tiled = jnp.tile(flipped, (1, block_len))
    shaped = tiled[:, : block_len * (2 * block_len - 1)].reshape(
        groups, block_len, 2 * block_len - 1
    )
    return shaped[:, :, block_len - 1 :]


def diag_sum(prods):
    groups, block_len, _ = prods.shape
    padded = jnp.pad(prods, ((0, 0), (0, 0), (block_len - 1, 0)))
    flat = padded.reshape(groups, block_len * (2 * block_len - 1))
    flat = jnp.pad(flat, ((0, 0), (0, block_len)))
    sums = flat.reshape(groups, block_len, 2 * block_len).sum(axis=1)
    return sums[:, ::-1].T


def add_window(tap_sums, window_grad, offset, block_len):
    current = lax.dynamic_slice_in_dim(tap_sums, offset * block_len, 2 * block_len, 0)
    return lax.dynamic_update_slice_in_dim(tap_sums, current + window_grad, offset * block_len, 0)


def kernel_block(taps, limits, offset, block_len):
    window = lax.dynamic_slice_in_dim(taps, offset * block_len, 2 * block_len, 0)
    weights = offset < limits
    tmat = toeplitz(window) * weights.astype(jnp.bfloat16)[:, None, None]
    return (tmat, weights.astype(jnp.float32))


def body(query_seq, key_seq, value_seq, out_grad, filters, skip_gain, reaches):
    f32 = jnp.float32
    block_len = query_seq.shape[0]
    local_width = query_seq.shape[1]
    local_groups = local_width // GROUP
    num_spans = lax.axis_size("ctx")
    seq_len = block_len * num_spans
    scale = 1.0 / math.sqrt(seq_len)
    myself = lax.axis_index("ctx")
    z_vals = (key_seq.astype(f32) * value_seq.astype(f32)).astype(jnp.bfloat16)
    grads = (out_grad.astype(f32) * query_seq.astype(f32)).astype(jnp.bfloat16)
    all_taps = lax.all_gather(filters, "ctx", axis=0, tiled=True)
    taps = jnp.concatenate([jnp.zeros((block_len, local_groups), jnp.bfloat16), all_taps], axis=0)
    longest = jnp.max(reaches)
    own_grads = grads.reshape(block_len, local_groups, GROUP)
    start = (
        jnp.zeros((block_len, local_groups, GROUP), f32),
        jnp.zeros((block_len, local_groups, GROUP), f32),
        jnp.zeros((seq_len + block_len, local_groups), f32),
    )
    z_piece = lax.all_gather(z_vals, "ctx", axis=0, tiled=True)
    g_piece = lax.all_gather(grads, "ctx", axis=0, tiled=True)
    count = z_piece.shape[0] // block_len

    def span_step(position, state):
        filtered, back_sum, tap_sums = state
        remote_z = lax.dynamic_slice_in_dim(z_piece, position * block_len, block_len, 0)
        remote_z = remote_z.reshape(block_len, local_groups, GROUP)
        remote_g = lax.dynamic_slice_in_dim(g_piece, position * block_len, block_len, 0)
        remote_g = remote_g.reshape(block_len, local_groups, GROUP)
        ahead = myself - position
        behind = position - myself

        def forward(inner):
            acc, sums = inner
            tmat, weights = kernel_block(taps, reaches, ahead, block_len)
            acc = acc + jnp.einsum("gab,bgc->agc", tmat, remote_z, preferred_element_type=f32)
            prods = jnp.einsum("agc,bgc->gab", own_grads, remote_z, preferred_element_type=f32)
            prods = prods * weights[:, None, None]
            return (acc, add_window(sums, diag_sum(prods), ahead, block_len))

        filtered, tap_sums = lax.cond(
            (ahead >= 0) & (ahead < longest), forward, lambda inner: inner, (filtered, tap_sums)
        )

        def backward(acc):
            tmat, weights = kernel_block(taps, reaches, behind, block_len)
            return acc + jnp.einsum("gab,agc->bgc", tmat, remote_g, preferred_element_type=f32)

        back_sum = lax.cond((behind >= 0) & (behind < longest), backward, lambda acc: acc, back_sum)
        return (filtered, back_sum, tap_sums)

    filtered, back_sum, tap_sums = lax.fori_loop(0, count, span_step, start)
    filtered = filtered.reshape(block_len, local_width)
    back_sum = back_sum.reshape(block_len, local_width)
    filter_grad = (
        lax.psum_scatter(tap_sums[block_len:], "ctx", scatter_dimension=0, tiled=True) * scale
    )
    skip_grad = lax.psum(jnp.sum(grads.astype(f32) * z_vals.astype(f32), axis=0), "ctx")
    filtered = filtered * scale
    back_sum = back_sum * scale
    total = filtered + skip_gain[None, :] * z_vals.astype(f32)
    mixed = (query_seq.astype(f32) * total).astype(jnp.bfloat16)
    query_grad = (out_grad.astype(f32) * total).astype(jnp.bfloat16)
    back_total = back_sum + skip_gain[None, :] * grads.astype(f32)
    key_grad = (back_total * value_seq.astype(f32)).astype(jnp.bfloat16)
    value_grad = (back_total * key_seq.astype(f32)).astype(jnp.bfloat16)
    return (mixed, query_grad, key_grad, value_grad, filter_grad, skip_grad)


def solution(mesh):
    in_specs = (
        P("ctx", "ch"),
        P("ctx", "ch"),
        P("ctx", "ch"),
        P("ctx", "ch"),
        P("ctx", "ch"),
        P("ch"),
        P("ch"),
    )
    out_specs = (
        P("ctx", "ch"),
        P("ctx", "ch"),
        P("ctx", "ch"),
        P("ctx", "ch"),
        P("ctx", "ch"),
        P("ch"),
    )
    return jax.shard_map(body, mesh=mesh, in_specs=in_specs, out_specs=out_specs, check_vma=False)
```

profile of v0, /device:TPU:8, one launch (start us, length us, event | category | flops | bytes accessed | tf_op | source)
XLA Modules:
  0.0 960.7 jit_solution(9368183063505255978)
XLA Ops:
  14.0 55.2 %all_gather.9 = bf16[4096,16]{0,1:T(8,128)(2,1)S(1)} all-gather(bf16[128,16]{0,1:T(8,128)(2,1)} %param.17), channel_id=1, replica_groups=mesh['ctx'=32,'ch'=16] {'ctx'}, dimensions={0}, use_global_device_ids=true | all-gather | bytes 135168 | tf_op jit(solution)/shard_map/all_gather | solution.py:53
  69.9 28.0 %all-gather.3.cloned.1.call-done = bf16[4096,256]{0,1:T(8,128)(2,1)} async-done(((bf16[128,256]{0,1:T(8,128)(2,1)}), bf16[4096,256]{0,1:T(8,128)(2,1)}) %all-gather.3.cloned.1.call-update) | async-done | bytes 2097168 | tf_op jit(solution)/shard_map/all_gather | solution.py:62
  97.9 83.6 %all-gather.5.cloned.1.call-done = bf16[4096,256]{0,1:T(8,128)(2,1)} async-done(((bf16[128,256]{0,1:T(8,128)(2,1)}), bf16[4096,256]{0,1:T(8,128)(2,1)}) %all-gather.5.cloned.1.call-update) | async-done | bytes 2097168 | tf_op jit(solution)/shard_map/all_gather | solution.py:63
  182.2 303.9 %while.20 = (s32[]{:T(128)}, f32[128,16,16]{0,2,1:T(8,128)S(1)}, f32[128,16,16]{0,2,1:T(8,128)}, f32[4224,16]{0,1:T(8,128)S(1)}, s32[]{:T(128)}, /*index=5*/s32[...) while((s32[]{:T(128)}, f32[128,16,16]{0,2,1:T(8,128)S(1)}, ...), condition=%wide.region_7.8_spmd, body=%wide.region_1.7_spmd.sunk | while | flops 27328612 | bytes 39176128 | solution.py:94
  183.5 8.4 conditional.5
  192.0 15.6 %conditional.4 = ((f32[128,16,16]{0,2,1:T(8,128)S(1)}, f32[4224,16]{0,1:T(8,128)S(1)})) conditional(s32[]{:T(128)} %convert_element_type.145, (f32[128,16,16]{0,2,1:T(8,128)S(1)}, f32[4224,16]{0,1:T(8,128)S(1)}) %tuple.66, (s32[]{:T(128)}, bf16[4224,16]{0,1:T(8,128)(2,1)}, s32[16]{0:T(128)}, bf16[4096,256]{0,1:T(8,128)(2,1)}, s32[]{:T(128)}, ...), branch_computations={%region_2.0_spmd, %region_3.4_spmd} | conditional | flops 17858612 | bytes 30565238 | solution.py:83
  208.8 8.4 conditional.5
  218.6 8.4 conditional.5
  228.3 8.4 conditional.5
  238.0 8.4 conditional.5
  247.7 8.4 conditional.5
  257.4 8.4 conditional.5
  267.2 8.4 conditional.5
  276.9 8.4 conditional.5
  286.6 8.4 conditional.5
  296.3 8.4 conditional.5
  306.1 8.4 conditional.5
  315.8 8.4 conditional.5
  325.5 8.4 conditional.5
  335.2 8.4 conditional.5
  432.5 8.4 conditional.5
  461.6 8.4 conditional.5
  486.9 311.9 %psum.7 = f32[256]{0:T(256)} all-reduce(f32[256]{0:T(256)S(1)} %get-tuple-element.328), channel_id=1, replica_groups=mesh['ctx'=32,'ch'=16] {'ctx'}, use_global_device_ids=true, to_apply=%region_10.11 | all-reduce | flops 256 | bytes 2048 | tf_op jit(solution)/shard_map/psum | solution.py:100
  803.8 149.0 %reduce-scatter.2.cloned.1.call-done = f32[128,16]{0,1:T(8,128)} async-done(((f32[4096,16]{0,1:T(8,128)}), f32[128,16]{0,1:T(8,128)}) %reduce-scatter.2.cloned.1.call-update) | async-done | bytes 8208 | tf_op jit(solution)/shard_map/reduce_scatter | solution.py:98
  (427 shorter events, 378.6 us)
Async XLA Ops:
  7.2 90.8 %all-gather.3.cloned.1.call-start = ((), (), s32[]{:S(2)}) async-start(), calls=%async_computation.1 | async-start | bytes 2162688 | tf_op jit(solution)/shard_map/all_gather | solution.py:62
  8.2 174.0 %copy-start.1 = (bf16[128,256]{0,1:T(8,128)(2,1)}, bf16[128,256]{0,1:T(8,128)(2,1)S(1)}, u32[]{:S(2)}) copy-start(bf16[128,256]{0,1:T(8,128)(2,1)S(1)} %copy.19) | copy-start | bytes 196612
  9.2 173.0 %copy-start.2 = (bf16[128,256]{0,1:T(8,128)(2,1)}, bf16[128,256]{0,1:T(8,128)(2,1)S(1)}, u32[]{:S(2)}) copy-start(bf16[128,256]{0,1:T(8,128)(2,1)S(1)} %copy.20) | copy-start | bytes 196612
  10.2 172.0 %copy-start.3 = (bf16[128,256]{0,1:T(8,128)(2,1)}, bf16[128,256]{0,1:T(8,128)(2,1)S(1)}, u32[]{:S(2)}) copy-start(bf16[128,256]{0,1:T(8,128)(2,1)S(1)} %copy.21) | copy-start | bytes 196612
  11.1 171.0 %copy-start.4 = (bf16[128,256]{0,1:T(8,128)(2,1)}, bf16[128,256]{0,1:T(8,128)(2,1)S(1)}, u32[]{:S(2)}) copy-start(bf16[128,256]{0,1:T(8,128)(2,1)S(1)} %copy.22) | copy-start | bytes 196612
  11.9 169.6 %all-gather.5.cloned.1.call-start = ((), (), s32[]{:S(2)}) async-start(), calls=%async_computation.2 | async-start | bytes 2162688 | tf_op jit(solution)/shard_map/all_gather | solution.py:63
  12.6 940.2 %reduce-scatter.2.cloned.1.call-start = ((), (), s32[]{:S(2)}) async-start(), calls=%async_computation.3 | async-start | bytes 270336 | tf_op jit(solution)/shard_map/reduce_scatter | solution.py:98
  182.2 617.4 %copy-start.7 = (f32[256]{0:T(256)S(1)}, f32[256]{0:T(256)}, u32[]{:S(2)}) copy-start(f32[256]{0:T(256)} %param.18) | copy-start | bytes 3076
  183.5 8.5 copy-start
  208.8 8.5 copy-start
  218.5 8.5 copy-start
  228.3 8.5 copy-start
  238.0 8.5 copy-start
  247.7 8.5 copy-start
  257.4 8.5 copy-start
  267.2 8.5 copy-start
  276.9 8.5 copy-start
  296.3 8.5 copy-start
  306.1 8.5 copy-start
  315.8 8.5 copy-start
  325.5 8.5 copy-start
  335.2 8.5 copy-start
  344.9 8.5 copy-start
  461.6 8.5 copy-start
  (18 other events, 115.8 us)
Sparse Core Ops, SparseCore 0:
  12.0 85.8 all-gather.2
  101.6 79.9 all-gather.4
  487.0 465.8 reduce-scatter.1
where the time goes:
time: 969 us; the launch traced here: 961 us
  blocking collectives  367 us (38%)
  waiting for transfers between devices  261 us (27%)
  local copies, waits for them, and re-layouts  193 us (20%)
  matrix products  58 us (6%)
  loops' own time  42 us (4%)
  other arithmetic  25.4 us (3%)
  between operations  13.9 us (1%)
    psum x1, blocking collectives, body(): lax.psum(jnp.sum(grads.astype(f32) * z_vals.astype(f32), axis=0), 'ctx')  312 us
    reduce_scatter x1, waiting for transfers between devices, body(): lax.psum_scatter(tap_sums[block_len:], 'ctx', scatter_dimension=0, tiled=...  149 us
    reshape x30, local copies, waits for them, and re-layouts, toeplitz(): tiled[:, :block_len * (2 * block_len - 1)]  102 us
    all_gather x1, waiting for transfers between devices, body(): g_piece = lax.all_gather(grads, 'ctx', axis=0, tiled=True)  83.6 us
    dot_general x29, matrix products, backward(): jnp.einsum('gab,agc->bgc', tmat, remote_g, preferred_element_type=f32)  55.6 us
    all_gather x1, blocking collectives, body(): all_taps = lax.all_gather(filters, 'ctx', axis=0, tiled=True)  55.2 us
    another operation x1, loops' own time, body(): filtered, back_sum, tap_sums = lax.fori_loop(0, count, span_step, start)  40.6 us
    all_gather x1, waiting for transfers between devices, body(): z_piece = lax.all_gather(z_vals, 'ctx', axis=0, tiled=True)  28 us
  transfers between devices with their start and end apart: 3, of which 3 were waited for; matrix products, arithmetic and copies ran while one was open for 1% of the time, Pallas kernels for 0%

commit v1 on v0

--- a/solution.py
+++ b/solution.py
@@ -59,8 +59,11 @@
         jnp.zeros((block_len, local_groups, GROUP), f32),
         jnp.zeros((seq_len + block_len, local_groups), f32),
     )
-    z_piece = lax.all_gather(z_vals, "ctx", axis=0, tiled=True)
-    g_piece = lax.all_gather(grads, "ctx", axis=0, tiled=True)
+    z_piece, g_piece = jnp.split(
+        lax.all_gather(jnp.concatenate([z_vals, grads], axis=1), "ctx", axis=0, tiled=True),
+        [z_vals.shape[1]],
+        axis=1,
+    )
     count = z_piece.shape[0] // block_len
 
     def span_step(position, state):

time: 969 us -> 856 us (0.88)
  waiting for transfers between devices: 261 us -> 185 us
  other arithmetic: 25.4 us -> 5.7 us
  blocking collectives: 367 us -> 348 us
    all_gather x2 -> x1, waiting for transfers between devices: 112 us -> 36.6 us  [body(): lax.all_gather(jnp.concatenate([z_vals, grads], axis=1), 'ctx', axis=0, t...]
    psum x1, blocking collectives: 312 us -> 293 us  [body(): lax.psum(jnp.sum(grads.astype(f32) * z_vals.astype(f32), axis=0), 'ctx')]
    convert_element_type x29, other arithmetic: 19.2 us -> 0.14 us  [kernel_block(): tmat = toeplitz(window) * weights.astype(jnp.bfloat16)[:, None, None]]
  transfers between devices with their start and end apart: 3 -> 2, of which waited for: 3 -> 2; matrix products, arithmetic and copies ran while one was open for 1% -> 1% of each run, Pallas kernels for 0% -> 0%
where the time goes in v1:
time: 856 us; the launch traced here: 849 us
  blocking collectives  348 us (41%)
  local copies, waits for them, and re-layouts  196 us (23%)
  waiting for transfers between devices  185 us (22%)
  matrix products  58 us (7%)
  loops' own time  42.6 us (5%)
  between operations  14.2 us (2%)
    psum x1, blocking collectives, body(): lax.psum(jnp.sum(grads.astype(f32) * z_vals.astype(f32), axis=0), 'ctx')  293 us
    reduce_scatter x1, waiting for transfers between devices, body(): lax.psum_scatter(tap_sums[block_len:], 'ctx', scatter_dimension=0, tiled=...  148 us
    reshape x30, local copies, waits for them, and re-layouts, toeplitz(): tiled[:, :block_len * (2 * block_len - 1)]  102 us
    dot_general x29, matrix products, backward(): jnp.einsum('gab,agc->bgc', tmat, remote_g, preferred_element_type=f32)  55.6 us
    all_gather x1, blocking collectives, body(): all_taps = lax.all_gather(filters, 'ctx', axis=0, tiled=True)  55.3 us
    another operation x1, loops' own time, body(): filtered, back_sum, tap_sums = lax.fori_loop(0, count, span_step, start)  41 us
    all_gather x1, waiting for transfers between devices, body(): lax.all_gather(jnp.concatenate([z_vals, grads], axis=1), 'ctx', axis=0, t...  36.6 us
    dynamic_slice x29, local copies, waits for them, and re-layouts, span_step(): lax.dynamic_slice_in_dim(g_piece, position * block_len, block_len, 0)  24.5 us
  transfers between devices with their start and end apart: 2, of which 2 were waited for; matrix products, arithmetic and copies ran while one was open for 1% of the time, Pallas kernels for 0%

profile of v1, /device:TPU:8, one launch (start us, length us, event | category | flops | bytes accessed | tf_op | source)
XLA Modules:
  0.0 849.1 jit_solution(16423132895359161047)
XLA Ops:
  14.0 55.3 %all_gather.6 = bf16[4096,16]{0,1:T(8,128)(2,1)S(1)} all-gather(bf16[128,16]{0,1:T(8,128)(2,1)} %param.17), channel_id=1, replica_groups=mesh['ctx'=32,'ch'=16] {'ctx'}, dimensions={0}, use_global_device_ids=true | all-gather | bytes 135168 | tf_op jit(solution)/shard_map/all_gather | solution.py:53
  69.9 36.6 %all-gather.2.cloned.1.call-done = bf16[4096,512]{0,1:T(8,128)(2,1)} async-done(((bf16[128,512]{0,1:T(8,128)(2,1)}), bf16[4096,512]{0,1:T(8,128)(2,1)}) %all-gather.2.cloned.1.call-update) | async-done | bytes 4194320 | tf_op jit(solution)/shard_map/all_gather | solution.py:63
  111.9 282.6 %while.20 = (s32[]{:T(128)}, f32[128,16,16]{0,2,1:T(8,128)S(1)}, f32[128,16,16]{0,2,1:T(8,128)}, f32[4224,16]{0,1:T(8,128)S(1)}, s32[]{:T(128)}, /*index=5*/s32[...) while((s32[]{:T(128)}, f32[128,16,16]{0,2,1:T(8,128)S(1)}, ...), condition=%wide.region_7.8_spmd, body=%wide.region_1.7_spmd.sunk | while | flops 27328612 | bytes 38913960 | solution.py:97
  113.2 7.8 conditional.5
  121.0 15.0 %conditional.4 = ((f32[128,16,16]{0,2,1:T(8,128)S(1)}, f32[4224,16]{0,1:T(8,128)S(1)})) conditional(s32[]{:T(128)} %convert_element_type.145, (f32[128,16,16]{0,2,1:T(8,128)S(1)}, f32[4224,16]{0,1:T(8,128)S(1)}) %tuple.67, (s32[]{:T(128)}, bf16[4224,16]{0,1:T(8,128)(2,1)}, s32[16]{0:T(128)S(1)}, bf16[4096,256]{0,1:T(8,128)(2,1)}, s32[]{:T(128)}, ...), branch_computations={%region_2.0_spmd, %region_3.4_spmd} | conditional | flops 17858612 | bytes 30565238 | solution.py:86
  137.2 7.8 conditional.5
  146.3 7.8 conditional.5
  155.4 7.8 conditional.5
  164.5 7.8 conditional.5
  173.6 7.8 conditional.5
  182.7 7.8 conditional.5
  191.8 7.8 conditional.5
  219.0 7.8 conditional.5
  228.1 7.8 conditional.5
  255.4 7.8 conditional.5
  264.5 7.8 conditional.5
  273.6 7.8 conditional.5
  300.8 7.8 conditional.5
  309.9 7.8 conditional.5
  346.3 7.8 conditional.5
  373.5 7.8 conditional.5
  382.6 7.8 conditional.5
  395.2 292.8 %psum.7 = f32[256]{0:T(256)} all-reduce(f32[256]{0:T(256)S(1)} %get-tuple-element.328), channel_id=1, replica_groups=mesh['ctx'=32,'ch'=16] {'ctx'}, use_global_device_ids=true, to_apply=%region_10.11 | all-reduce | flops 256 | bytes 2048 | tf_op jit(solution)/shard_map/psum | solution.py:103
  693.0 148.0 %reduce-scatter.2.cloned.1.call-done = f32[128,16]{0,1:T(8,128)} async-done(((f32[4096,16]{0,1:T(8,128)}), f32[128,16]{0,1:T(8,128)}) %reduce-scatter.2.cloned.1.call-update) | async-done | bytes 8208 | tf_op jit(solution)/shard_map/reduce_scatter | solution.py:101
  (364 shorter events, 345.7 us)
Async XLA Ops:
  7.2 99.3 %all-gather.2.cloned.1.call-start = ((), (), s32[]{:S(2)}) async-start(), calls=%async_computation.1 | async-start | bytes 4325376 | tf_op jit(solution)/shard_map/all_gather | solution.py:63
  8.2 103.0 %copy-start = (bf16[128,256]{0,1:T(8,128)(2,1)}, bf16[128,256]{0,1:T(8,128)(2,1)S(1)}, u32[]{:S(2)}) copy-start(bf16[128,256]{0,1:T(8,128)(2,1)S(1)} %copy.19) | copy-start | bytes 196612
  9.2 102.0 %copy-start.1 = (bf16[128,256]{0,1:T(8,128)(2,1)}, bf16[128,256]{0,1:T(8,128)(2,1)S(1)}, u32[]{:S(2)}) copy-start(bf16[128,256]{0,1:T(8,128)(2,1)S(1)} %copy.20) | copy-start | bytes 196612
  10.2 101.0 %copy-start.2 = (bf16[128,256]{0,1:T(8,128)(2,1)}, bf16[128,256]{0,1:T(8,128)(2,1)S(1)}, u32[]{:S(2)}) copy-start(bf16[128,256]{0,1:T(8,128)(2,1)S(1)} %copy.21) | copy-start | bytes 196612
  11.1 100.0 %copy-start.3 = (bf16[128,256]{0,1:T(8,128)(2,1)}, bf16[128,256]{0,1:T(8,128)(2,1)S(1)}, u32[]{:S(2)}) copy-start(bf16[128,256]{0,1:T(8,128)(2,1)S(1)} %copy.22) | copy-start | bytes 196612
  11.3 0.6 copy-start.4
  12.6 828.4 %reduce-scatter.2.cloned.1.call-start = ((), (), s32[]{:S(2)}) async-start(), calls=%async_computation.2 | async-start | bytes 270336 | tf_op jit(solution)/shard_map/reduce_scatter | solution.py:101
  69.9 42.0 %copy-start.7 = (s32[16]{0:T(128)S(1)}, s32[16]{0:T(128)}, u32[]{:S(2)}) copy-start(s32[16]{0:T(128)} %param.19) | copy-start | bytes 196
  121.0 1.7 copy-start.5
  135.1 0.9 copy-start.6
Sparse Core Ops, SparseCore 0:
  12.7 93.7 all-gather.1
  395.3 445.6 reduce-scatter.1
